TPU v7x, 32 devices: a whole 2x2x4 slice. The times are simulated.
32 devices in a mesh: groups: 2 (over x), blk: 4 (over y, core), width: 4 (over z).
Axes of the slice: x: 2, y: 2, z: 4, core: 2. Of those that a mesh axis runs over, the one named last changes fastest.
Arguments:
- activations: float32 [8192, 8192], P(('groups', 'blk'), 'width'), parts along dimension 0, may hold values from -6 to 6
- query_grads: float32 [16, 8192, 128], P(('groups', 'blk'), 'width'), parts along dimension 0, may hold values from -0.0625 to 0.0625
- outgrad_proj: float32 [8192, 128], P(('groups', 'blk', 'width')), parts along dimension 0, may hold values from -0.6 to 0.6
- doc_ids: int32 [8192], P(('groups', 'blk', 'width')), parts along dimension 0, may hold values from 0 to 15, never falling along the last dimension, each value on 1 to 512 neighbouring positions
Outputs:
- token_scores: float32 [8192, 8], P(('groups', 'blk', 'width')), parts along dimension 0
- doc_scores: float32 [32, 8], P('groups'), parts along dimension 0
There are 2 independent parts, one for each index of `groups`. A program takes and returns all parts, laid end to end along the dimension named above; each array names one. Nothing has to cross between parts.
Inputs may be any that keep to these rules, and one draw needn't show every extreme that they name: `doc_ids`: never falls along the tokens; every document 0 to 15 holds 1 to 512 tokens, one exactly 512.
All inputs are finite; a program needn't handle non-finite values.
Results may differ from a plain program's by a relative error of at most 0.000078.
Values sent between devices are 32-bit elements; how exact they have to be, the bound alone decides.
No kernel may reach another device: no remote copies, remote signals or barrier semaphores. Data moves between devices by JAX's collectives and lax.ppermute only.
A program may use at most 128 MiB of HBM per device.

v0:
```python
import jax
import jax.numpy as jnp
from jax import lax
from jax.sharding import PartitionSpec as P

DOC_BLK = 4


def per_device(activations, query_grads, outgrad_proj, doc_ids):
    projected = jnp.einsum(
        "td,qdr->tqr",
        activations,
        lax.all_gather(query_grads, "blk", axis=0, tiled=True),
        precision=lax.Precision.HIGHEST,
        preferred_element_type=jnp.float32,
    )
    owned_parts = lax.psum_scatter(projected, "width", scatter_dimension=0, tiled=True)
    token_scores = jnp.sum(owned_parts * outgrad_proj[:, None, :], axis=2)
    doc_total = DOC_BLK * lax.axis_size("blk")
    doc_range = jnp.arange(doc_total, dtype=jnp.int32)
    onehot = (doc_ids[:, None] == doc_range[None, :]).astype(jnp.float32)
    doc_sums = jnp.einsum(
        "tn,tq->nq",
        onehot,
        token_scores,
        precision=lax.Precision.HIGHEST,
        preferred_element_type=jnp.float32,
    )
    doc_counts = jnp.sum(onehot, axis=0)
    doc_sums, doc_counts = lax.psum((doc_sums, doc_counts), ("blk", "width"))
    doc_scores = doc_sums / jnp.sqrt(doc_counts)[:, None]
    return (token_scores, doc_scores)


def solution(mesh):
    return jax.shard_map(
        per_device,
        mesh=mesh,
        in_specs=(
            P(("groups", "blk"), "width"),
            P(("groups", "blk"), "width", None),
            P(("groups", "blk", "width"), None),
            P(("groups", "blk", "width")),
        ),
        out_specs=(P(("groups", "blk", "width"), None), P("groups", None)),
        check_vma=False,
    )
```

profile of v0, /device:TPU:0, one launch (start us, length us, event | category | flops | bytes accessed | tf_op | source)
XLA Modules:
  0.0 222.9 jit_solution(11770008080408502427)
XLA Ops:
  7.2 0.0 all-gather.2.cloned.1.call-start
  7.2 0.7 all-gather.2.cloned.1.call-update
  7.9 0.0 copy-start.2
  7.9 0.0 copy-start
  7.9 0.0 reduce-scatter.2.cloned.1.call-start
  8.0 62.6 %all-gather.2.cloned.1.call-done = f32[8,2048,128]{2,1,0:T(8,128)} async-done(((f32[2,2048,128]{2,1,0:T(8,128)}), f32[8,2048,128]{2,1,0:T(8,128)}) %all-gather.2.cloned.1.call-update) | async-done | bytes 8388624 | tf_op jit(solution)/shard_map/all_gather | solution.py:13
  70.6 32.7 %fusion = f32[1024,8,128]{2,0,1:T(8,128)} fusion(f32[8,2048,128]{2,1,0:T(8,128)} %all-gather.2.cloned.1.call-done, f32[1024,2048]{1,0:T(8,128)} %param.4), kind=kOutput, calls=%fused_computation | convolution fusion | flops 25769803776 | bytes 20971520 | tf_op jit(solution)/shard_map/td,qdr->tqr/dot_general | solution.py:10
  103.3 0.0 reduce-scatter.2.cloned.1.call-update
  103.3 0.0 copy-done.2
  103.3 0.1 convert_reduce_fusion
  103.4 76.8 %reduce-scatter.2.cloned.1.call-done = f32[256,8,128]{2,0,1:T(8,128)} async-done(((f32[1024,8,128]{2,0,1:T(8,128)}), f32[256,8,128]{2,0,1:T(8,128)}) %reduce-scatter.2.cloned.1.call-update) | async-done | bytes 1048592 | tf_op jit(solution)/shard_map/reduce_scatter | solution.py:17
  180.2 0.0 copy-done
  180.2 1.6 multiply_reduce_fusion
  181.8 0.0 copy-start.1
  181.8 0.1 fusion.2
  181.9 33.5 %all-reduce = (f32[16,8]{0,1:T(8,128)S(1)}, f32[16]{0:T(128)S(1)}) all-reduce(f32[16,8]{0,1:T(8,128)S(1)} %fusion.2, f32[16]{0:T(128)S(1)} %convert_reduce_fusion), channel_id=1, replica_groups=mesh['groups'=2,'blk'=4,'width'=4] {'blk','width'}, use_global_device_ids=true, to_apply=%region_2.0 | all-reduce | flops 144 | bytes 1152 | tf_op jit(solution)/shard_map/psum | solution.py:30
  215.5 0.6 broadcast_divide_fusion
  216.1 0.0 copy-done.1
  (1 shorter events, 0.0 us)
Async XLA Ops:
  7.2 63.4 %all-gather.2.cloned.1.call-start = ((), (), s32[]{:S(2)}) async-start(), calls=%async_computation.1 | async-start | bytes 10485760 | tf_op jit(solution)/shard_map/all_gather | solution.py:13
  7.9 95.4 %copy-start.2 = (s32[256]{0:T(256)S(1)}, s32[256]{0:T(256)}, u32[]{:S(2)}) copy-start(s32[256]{0:T(256)} %param.7) | copy-start | bytes 3076
  7.9 172.3 %copy-start = (f32[256,128]{1,0:T(8,128)S(1)}, f32[256,128]{1,0:T(8,128)}, u32[]{:S(2)}) copy-start(f32[256,128]{1,0:T(8,128)} %param.6) | copy-start | bytes 393220
  7.9 172.3 %reduce-scatter.2.cloned.1.call-start = ((), (), s32[]{:S(2)}) async-start(), calls=%async_computation.2 | async-start | bytes 5242880 | tf_op jit(solution)/shard_map/reduce_scatter | solution.py:17
  181.8 34.3 %copy-start.1 = (f32[256,8]{0,1:T(8,128)}, f32[256,8]{0,1:T(8,128)S(1)}, u32[]{:S(2)}) copy-start(f32[256,8]{0,1:T(8,128)S(1)} %multiply_reduce_fusion) | copy-start | bytes 24580
Sparse Core Ops, SparseCore 0:
  9.6 60.9 all-gather.1
  103.4 76.7 reduce-scatter.1
where the time goes:
time: 223 us
  waiting for transfers between devices  140 us (63%)
  blocking collectives  33.5 us (15%)
  matrix products  32.8 us (15%)
  between operations  14.1 us (6%)
  other arithmetic  2.29 us (1%)
    reduce_scatter x1, waiting for transfers between devices, per_device(): lax.psum_scatter(projected, 'width', scatter_dimension=0, tiled=True)  76.8 us
    all_gather x1, waiting for transfers between devices, per_device(): lax.all_gather(query_grads, 'blk', axis=0, tiled=True)  62.6 us
    psum x1, blocking collectives, per_device(): doc_sums, doc_counts = lax.psum((doc_sums, doc_counts), ('blk', 'width'))  33.5 us
    dot_general x1, matrix products, per_device(): jnp.einsum('td,qdr->tqr', activations, lax.all_gather(query_grads, 'blk',...  32.7 us
  transfers between devices with their start and end apart: 2, of which 2 were waited for; matrix products, arithmetic and copies ran while one was open for 0% of the time, Pallas kernels for 0%

commit v1 on v0

v1 whole, which is shorter than its diff:
```python
import functools

import jax
import jax.numpy as jnp
from jax import lax
from jax.experimental import pallas as pl
from jax.experimental.pallas import tpu as pltpu
from jax.sharding import PartitionSpec as P

DOC_BLK = 4
LANES = 128
F32, BF16 = jnp.float32, jnp.bfloat16
VMEM = pl.BlockSpec(memory_space=pltpu.VMEM)
SMEM = pl.BlockSpec(memory_space=pltpu.SMEM)
LIMIT = 40 << 20


def split(x):
    high = x.astype(BF16)
    return high, (x - high.astype(F32)).astype(BF16)


def project(a, g):
    ah, al = split(a)
    gh, gl = split(g)
    dot = functools.partial(jnp.dot, preferred_element_type=F32)
    return dot(ah, gh) + dot(al, gh) + dot(ah, gl)


def score_rows(p, o, s_ref):
    r = o.shape[1]
    for i in range(s_ref.shape[0]):
        s_ref[i, :] = jnp.sum(p[:, i * r : (i + 1) * r] * o, axis=1)


def near_kernel(a_ref, g_ref, c_ref, o_ref, s_ref, acc_ref):
    k = pl.program_id(0)
    gs = [ref[q] for ref in (g_ref, c_ref) for q in range(ref.shape[0])]
    p = project(a_ref[...], jnp.concatenate(gs, axis=1))

    @pl.when(k == 0)
    def _():
        acc_ref[...] = p

    @pl.when(k > 0)
    def _():
        acc_ref[...] += p

    @pl.when(k == pl.num_programs(0) - 1)
    def _():
        score_rows(acc_ref[...], o_ref[...], s_ref)


def near_scores(a, g, c, o):
    t, d = a.shape
    nq, _, r = g.shape
    kc = min(d, 512)
    return pl.pallas_call(
        near_kernel,
        grid=(d // kc,),
        in_specs=[
            pl.BlockSpec((t, kc), lambda k: (0, k)),
            pl.BlockSpec((nq, kc, r), lambda k: (0, k, 0)),
            pl.BlockSpec((nq, kc, r), lambda k: (0, k, 0)),
            pl.BlockSpec((t, r), lambda k: (0, 0)),
        ],
        out_specs=pl.BlockSpec((2 * nq, t), lambda k: (0, 0)),
        out_shape=jax.ShapeDtypeStruct((2 * nq, t), F32),
        scratch_shapes=[pltpu.VMEM((t, 2 * nq * r), F32)],
        compiler_params=pltpu.CompilerParams(vmem_limit_bytes=LIMIT),
        cost_estimate=pl.CostEstimate(
            flops=12 * t * d * nq * r, bytes_accessed=4 * (t * d + 2 * nq * d * r), transcendentals=0
        ),
    )(a, g, c, o)


def far_kernel(a_ref, y_ref, c_ref, o_ref, prev_ref, s_ref):
    p = project(a_ref[...], jnp.concatenate([y_ref[...], c_ref[...]], axis=1))
    score_rows(p, o_ref[...], s_ref)
    s_ref[...] += prev_ref[...]


def far_specs(t, r, kc, at):
    return [
        pl.BlockSpec((t, kc), lambda i: (0, at)),
        pl.BlockSpec((kc, r), lambda i: (0, 0)),
        pl.BlockSpec((kc, r), lambda i: (0, 0)),
        pl.BlockSpec((t, r), lambda i: (0, 0)),
        pl.BlockSpec((2, t), lambda i: (0, 0)),
    ]


def far_cost(t, r, kc):
    return pl.CostEstimate(
        flops=12 * t * kc * r, bytes_accessed=4 * (t * kc + 2 * kc * r), transcendentals=0
    )


def far_scores(a, y, c, o, prev, start):
    t = a.shape[0]
    kc, r = y.shape
    return pl.pallas_call(
        far_kernel,
        grid=(1,),
        in_specs=far_specs(t, r, kc, start // kc),
        out_specs=pl.BlockSpec((2, t), lambda i: (0, 0)),
        out_shape=jax.ShapeDtypeStruct((2, t), F32),
        compiler_params=pltpu.CompilerParams(vmem_limit_bytes=LIMIT),
        cost_estimate=far_cost(t, r, kc),
    )(a, y, c, o, prev)


def per_device(a, g, o, ids):
    nb, nw = lax.axis_size("blk"), lax.axis_size("width")
    b, w = lax.axis_index("blk"), lax.axis_index("width")
    nq, d, r = g.shape
    t = a.shape[0]
    own = o.shape[0]
    docs = DOC_BLK * nb
    pairs = lambda n, k: [(i, i ^ k) for i in range(n)]
    to_core = lambda x: lax.ppermute(x, "blk", pairs(nb, 1))

    sizes = [d // 4] * 4
    pieces = []
    for q in range(nq):
        at = 0
        for n in sizes:
            pieces.append((q, at, n))
            at += n
    arrived = {}
    for j in range(2, nb, 2):
        for q, at, n in pieces:
            arrived[j, q, at] = lax.ppermute(g[q, at : at + n], "blk", pairs(nb, j))
    core = to_core(g)

    rows = own // LANES
    flat = ids.astype(F32).reshape(rows, LANES)
    mine = jnp.concatenate([o, flat], axis=0)
    all_o = jnp.zeros((t, r), F32)
    all_ids = jnp.zeros((t // LANES, LANES), F32)
    for k in range(nw):
        got = lax.ppermute(mine, "width", pairs(nw, k)) if k else mine
        src = w ^ k
        all_o = lax.dynamic_update_slice(all_o, got[:own], (src * own, 0))
        all_ids = lax.dynamic_update_slice(all_ids, got[own:], (src * rows, 0))

    near = near_scores(a, g, core, all_o)
    scores = {0: near[:nq], 1: near[nq:]}
    for j in range(2, nb, 2):
        per_q = []
        for q in range(nq):
            s = jnp.zeros((2, t), F32)
            for q2, at, n in pieces:
                if q2 == q:
                    y = arrived[j, q, at]
                    s = far_scores(a, y, to_core(y), all_o, s, at)
            per_q.append(s)
        scores[j] = jnp.stack([s[0] for s in per_q])
        scores[j + 1] = jnp.stack([s[1] for s in per_q])

    blocks = [scores[k] for k in range(nb)]
    bit = 1
    while bit < nb:
        swap = (b & bit) != 0
        blocks = [jnp.where(swap, blocks[i ^ bit], blocks[i]) for i in range(nb)]
        bit *= 2
    s = jnp.concatenate(blocks, axis=0)

    token_ids = all_ids.reshape(t)
    ndoc = jnp.arange(docs, dtype=F32)
    onehot = (token_ids[:, None] == ndoc[None, :]).astype(F32)
    doc = jnp.dot(s, onehot, precision=lax.Precision.HIGHEST, preferred_element_type=F32)
    count = jnp.sum((ids[:, None] == jnp.arange(docs, dtype=jnp.int32)[None, :]).astype(F32), axis=0)
    doc = jnp.concatenate([doc, jnp.broadcast_to(count[None, :], doc.shape)], axis=1)

    k = 1
    while k < nb:
        doc = doc + lax.ppermute(doc, "blk", pairs(nb, k))
        k *= 2
    k = nw // 2
    while k:
        half = s.shape[1] // 2
        low = (w & k) == 0
        keep = jnp.where(low, s[:, :half], s[:, half:])
        send = jnp.where(low, s[:, half:], s[:, :half])
        got = lax.ppermute(jnp.concatenate([send, doc], axis=1), "width", pairs(nw, k))
        s = keep + got[:, :half]
        doc = doc + got[:, half:]
        k //= 2
    doc_scores = (doc[:, :docs] / jnp.sqrt(doc[:, docs:])).T
    return (s.T, doc_scores)


def solution(mesh):
    return jax.shard_map(
        per_device,
        mesh=mesh,
        in_specs=(
            P(("groups", "blk"), "width"),
            P(("groups", "blk"), "width", None),
            P(("groups", "blk", "width"), None),
            P(("groups", "blk", "width")),
        ),
        out_specs=(P(("groups", "blk", "width"), None), P("groups", None)),
        check_vma=False,
    )
```

time: 223 us -> 99 us (0.44)
  waiting for transfers between devices: 140 us -> 40.7 us
  blocking collectives: 33.5 us -> 0 us
  matrix products: 32.8 us -> 0.37 us
  starting transfers between devices: 0.08 us -> 23.4 us
  Pallas kernels: 0 us -> 18.1 us
  between operations: 14.1 us -> 0.89 us
  local copies, waits for them, and re-layouts: 0.02 us -> 11.3 us
    reduce_scatter x1 -> x0, waiting for transfers between devices: 76.8 us -> none  [per_device(): lax.psum_scatter(projected, 'width', scatter_dimension=0, tiled=True)]
    all_gather x1 -> x0, waiting for transfers between devices: 62.6 us -> none  [per_device(): lax.all_gather(query_grads, 'blk', axis=0, tiled=True)]
    ppermute x0 -> x24, waiting for transfers between devices: none -> 40.7 us  [the longest x8 29.5 us: per_device(): arrived[j, q, at] = lax.ppermute(g[q, at:at + n], 'blk', pairs(nb, j))]
    psum x1 -> x0, blocking collectives: 33.5 us -> none  [per_device(): doc_sums, doc_counts = lax.psum((doc_sums, doc_counts), ('blk', 'width'))]
    dot_general x2 -> x1, matrix products: 32.8 us -> 0.37 us  [per_device(): jnp.dot(s, onehot, precision=lax.Precision.HIGHEST, preferred_element_typ...]
    ppermute x0 -> x24, starting transfers between devices: none -> 23.4 us  [the longest x8 10.4 us: per_device(): arrived[j, q, at] = lax.ppermute(g[q, at:at + n], 'blk', pairs(nb, j))]
    pallas_call x0 -> x9, Pallas kernels: none -> 18.1 us  [the longest x1 9.4 us: near_scores(): pl.pallas_call(near_kernel, grid=(d // kc,), in_specs=[pl.BlockSpec((t, k...]
    dynamic_update_slice x0 -> x7, local copies, waits for them, and re-layouts: none -> 4.81 us  [the longest x4 2.76 us: per_device(): all_o = lax.dynamic_update_slice(all_o, got[:own], (src * own, 0))]
  transfers between devices with their start and end apart: 2 -> 24, of which waited for: 2 -> 12; matrix products, arithmetic and copies ran while one was open for 0% -> 8% of each run, Pallas kernels for 0% -> 9%
where the time goes in v1:
time: 99 us; the launch traced here: 98.7 us
  waiting for transfers between devices  40.7 us (41%)
  starting transfers between devices  23.4 us (24%)
  Pallas kernels  18.1 us (18%)
  local copies, waits for them, and re-layouts  11.3 us (11%)
  other arithmetic  3.78 us (4%)
    ppermute x8, waiting for transfers between devices, per_device(): arrived[j, q, at] = lax.ppermute(g[q, at:at + n], 'blk', pairs(nb, j))  29.5 us
    ppermute x8, starting transfers between devices, per_device(): arrived[j, q, at] = lax.ppermute(g[q, at:at + n], 'blk', pairs(nb, j))  10.4 us
    pallas_call x1, Pallas kernels, near_scores(): pl.pallas_call(near_kernel, grid=(d // kc,), in_specs=[pl.BlockSpec((t, k...  9.4 us
    pallas_call x8, Pallas kernels, far_scores(): pl.pallas_call(far_kernel, grid=(1,), in_specs=far_specs(t, r, kc, start...  8.69 us
    ppermute x3, starting transfers between devices, per_device(): got = lax.ppermute(mine, 'width', pairs(nw, k)) if k else mine  5.68 us
    ppermute x2, waiting for transfers between devices, per_device(): lax.ppermute(jnp.concatenate([send, doc], axis=1), 'width', pairs(nw, k))  4.66 us
    ppermute x2, starting transfers between devices, per_device(): lax.ppermute(jnp.concatenate([send, doc], axis=1), 'width', pairs(nw, k))  3.84 us
    unnamed x8, local copies, waits for them, and re-layouts  3.84 us
  transfers between devices with their start and end apart: 24, of which 12 were waited for; matrix products, arithmetic and copies ran while one was open for 8% of the time, Pallas kernels for 9%

profile of v1, /device:TPU:0, one launch (start us, length us, event | category | flops | bytes accessed | tf_op | source)
XLA Modules:
  0.0 98.7 jit_solution(1723120721342047674)
XLA Ops:
  0.6 0.7 convert_bitcast_fusion
  1.3 1.6 %pad_maximum_fusion = f32[258,128]{1,0:T(8,128)} fusion(f32[2,128]{1,0:T(2,128)S(1)} %convert_bitcast_fusion, f32[256,128]{1,0:T(8,128)} %param.6), kind=kLoop, calls=%fused_computation.11 | loop fusion | flops 33024 | bytes 264192 | tf_op jit(solution)/shard_map/concatenate | solution.py:138
  2.9 5.0 %collective-permute-start.4 = (f32[258,128]{1,0:T(8,128)}, f32[258,128]{1,0:T(8,128)}, u32[]{:S(2)}, u32[]{:S(2)}) collective-permute-start(f32[258,128]{1,0:T(8,128)} %pad_maximum_fusion), channel_id=1, source_target_pairs={{0,3},{1,2},{2,1},{3,0},{4,7},{5,6},{6,5},{7,4},{8,11},{9,10},{10,... | collective-permute-start | bytes 396296 | tf_op jit(solution)/shard_map/ppermute | solution.py:142
  7.9 0.0 collective-permute-start.3
  7.9 0.6 collective-permute-start.2
  8.6 0.0 collective-permute-start.19
  8.6 2.6 %slice_bitcast_fusion.4 = (f32[512,128]{1,0:T(8,128)}, f32[512,128]{1,0:T(8,128)}, f32[512,128]{1,0:T(8,128)}, f32[512,128]{1,0:T(8,128)}, f32[512,128]{1,0:T(8,...) fusion(f32[2,2048,128]{2,1,0:T(8,128)} %g_ref.1), kind=kLoop, calls=%fused_computation.7 | loop fusion | bytes 4194304 | tf_op jit(solution)/shard_map/squeeze | solution.py:133
  11.1 1.7 %collective-permute-start.9 = (f32[512,128]{1,0:T(8,128)}, f32[512,128]{1,0:T(8,128)S(1)}, u32[]{:S(2)}, u32[]{:S(2)}) collective-permute-start(f32[512,128]{1,0:T(8,128)} %get-tuple-element.2), channel_id=1, source_target_pairs={{0,8},{4,12},{8,0},{12,4},{1,9},{5,13},{9,1},{13,5},{2,10},{6,14},... | collective-permute-start | bytes 786440 | tf_op jit(solution)/shard_map/ppermute | solution.py:133
  12.8 0.1 convert_reduce_fusion
  13.0 0.1 pad.5.clone
  13.1 3.8 %collective-permute-done.2 = f32[258,128]{1,0:T(8,128)} collective-permute-done((f32[258,128]{1,0:T(8,128)}, f32[258,128]{1,0:T(8,128)}, u32[]{:S(2)}, u32[]{:S(2)}) %collective-permute-start.2) | collective-permute-done | bytes 132128 | tf_op jit(solution)/shard_map/ppermute | solution.py:142
  16.9 1.5 %collective-permute-start.17 = (f32[512,128]{1,0:T(8,128)}, f32[512,128]{1,0:T(8,128)S(1)}, u32[]{:S(2)}, u32[]{:S(2)}) collective-permute-start(f32[512,128]{1,0:T(8,128)} %get-tuple-element.3), channel_id=1, source_target_pairs={{0,8},{4,12},{8,0},{12,4},{1,9},{5,13},{9,1},{13,5},{2,10},{6,14},... | collective-permute-start | bytes 786440 | tf_op jit(solution)/shard_map/ppermute | solution.py:133
  18.5 0.9 slice_dynamic-update-slice_fusion.2
  19.4 0.6 collective-permute-start.15
  20.0 0.0 collective-permute-done.3
  20.0 1.5 %collective-permute-start.13 = (f32[512,128]{1,0:T(8,128)}, f32[512,128]{1,0:T(8,128)S(1)}, u32[]{:S(2)}, u32[]{:S(2)}) collective-permute-start(f32[512,128]{1,0:T(8,128)} %get-tuple-element.5), channel_id=1, source_target_pairs={{0,8},{4,12},{8,0},{12,4},{1,9},{5,13},{9,1},{13,5},{2,10},{6,14},... | collective-permute-start | bytes 786440 | tf_op jit(solution)/shard_map/ppermute | solution.py:133
  21.5 0.9 slice_dynamic-update-slice_fusion.1
  22.4 0.0 collective-permute-done.9.y_ref
  22.4 0.6 collective-permute-start.11
  23.0 0.9 slice_dynamic-update-slice_fusion.o_ref
  23.9 2.5 %collective-permute-done.17.y_ref = f32[512,128]{1,0:T(8,128)S(1)} collective-permute-done((f32[512,128]{1,0:T(8,128)}, f32[512,128]{1,0:T(8,128)S(1)}, u32[]{:S(2)}, u32[]{:S(2)}) %collective-permute-start.17) | collective-permute-done | bytes 262176 | tf_op jit(solution)/shard_map/ppermute | solution.py:133
  26.4 1.5 %collective-permute-start.7 = (f32[512,128]{1,0:T(8,128)S(1)}, f32[512,128]{1,0:T(8,128)S(1)}, u32[]{:S(2)}, u32[]{:S(2)}) collective-permute-start(f32[512,128]{1,0:T(8,128)S(1)} %get-tuple-element.7), channel_id=1, source_target_pairs={{0,8},{4,12},{8,0},{12,4},{1,9},{5,13},{9,1},{13,5},{2,10},{6,14},... | collective-permute-start | bytes 786440 | tf_op jit(solution)/shard_map/ppermute | solution.py:133
  27.9 4.1 %collective-permute-done.15.y_ref = f32[512,128]{1,0:T(8,128)S(1)} collective-permute-done((f32[512,128]{1,0:T(8,128)}, f32[512,128]{1,0:T(8,128)S(1)}, u32[]{:S(2)}, u32[]{:S(2)}) %collective-permute-start.15) | collective-permute-done | bytes 262176 | tf_op jit(solution)/shard_map/ppermute | solution.py:133
  32.0 1.5 %collective-permute-start.5 = (f32[512,128]{1,0:T(8,128)S(1)}, f32[512,128]{1,0:T(8,128)S(1)}, u32[]{:S(2)}, u32[]{:S(2)}) collective-permute-start(f32[512,128]{1,0:T(8,128)S(1)} %get-tuple-element.8), channel_id=1, source_target_pairs={{0,8},{4,12},{8,0},{12,4},{1,9},{5,13},{9,1},{13,5},{2,10},{6,14},... | collective-permute-start | bytes 786440 | tf_op jit(solution)/shard_map/ppermute | solution.py:133
  33.5 4.1 %collective-permute-done.13.y_ref = f32[512,128]{1,0:T(8,128)S(1)} collective-permute-done((f32[512,128]{1,0:T(8,128)}, f32[512,128]{1,0:T(8,128)S(1)}, u32[]{:S(2)}, u32[]{:S(2)}) %collective-permute-start.13) | collective-permute-done | bytes 262176 | tf_op jit(solution)/shard_map/ppermute | solution.py:133
  37.6 1.5 %collective-permute-start = (f32[512,128]{1,0:T(8,128)S(1)}, f32[512,128]{1,0:T(8,128)S(1)}, u32[]{:S(2)}, u32[]{:S(2)}) collective-permute-start(f32[512,128]{1,0:T(8,128)S(1)} %get-tuple-element.9), channel_id=1, source_target_pairs={{0,8},{4,12},{8,0},{12,4},{1,9},{5,13},{9,1},{13,5},{2,10},{6,14},... | collective-permute-start | bytes 786440 | tf_op jit(solution)/shard_map/ppermute | solution.py:133
  39.1 0.7 constant_dynamic-update-slice_fusion.2
  39.8 3.4 %collective-permute-done.11.y_ref = f32[512,128]{1,0:T(8,128)S(1)} collective-permute-done((f32[512,128]{1,0:T(8,128)S(1)}, f32[512,128]{1,0:T(8,128)S(1)}, u32[]{:S(2)}, u32[]{:S(2)}) %collective-permute-start.11) | collective-permute-done | bytes 262176 | tf_op jit(solution)/shard_map/ppermute | solution.py:133
  43.2 0.7 constant_dynamic-update-slice_fusion.1
  43.9 4.9 %collective-permute-done.7.y_ref = f32[512,128]{1,0:T(8,128)S(1)} collective-permute-done((f32[512,128]{1,0:T(8,128)S(1)}, f32[512,128]{1,0:T(8,128)S(1)}, u32[]{:S(2)}, u32[]{:S(2)}) %collective-permute-start.7) | collective-permute-done | bytes 262176 | tf_op jit(solution)/shard_map/ppermute | solution.py:133
  48.9 5.6 %collective-permute-done.5.y_ref = f32[512,128]{1,0:T(8,128)S(1)} collective-permute-done((f32[512,128]{1,0:T(8,128)S(1)}, f32[512,128]{1,0:T(8,128)S(1)}, u32[]{:S(2)}, u32[]{:S(2)}) %collective-permute-start.5) | collective-permute-done | bytes 262176 | tf_op jit(solution)/shard_map/ppermute | solution.py:133
  54.5 0.0 collective-permute-start.16
  54.5 4.9 %collective-permute-done.y_ref = f32[512,128]{1,0:T(8,128)S(1)} collective-permute-done((f32[512,128]{1,0:T(8,128)S(1)}, f32[512,128]{1,0:T(8,128)S(1)}, u32[]{:S(2)}, u32[]{:S(2)}) %collective-permute-start) | collective-permute-done | bytes 262176 | tf_op jit(solution)/shard_map/ppermute | solution.py:133
  59.4 0.7 constant_dynamic-update-slice_fusion
  60.1 0.5 collective-permute-start.12
  60.6 3.4 %copy-done = f32[1024,2048]{1,0:T(8,128)S(1)} copy-done((f32[1024,2048]{1,0:T(8,128)S(1)}, f32[1024,2048]{1,0:T(8,128)}, u32[]{:S(2)}) %copy-start) | copy-done | bytes 8388632
  64.0 1.1 %shard_map.59.prev_ref = f32[2,1024]{1,0:T(2,128)S(1)} custom-call(f32[1024,2048]{1,0:T(8,128)S(1)} %copy-done, f32[512,128]{1,0:T(8,128)S(1)} %collective-permute-done.9.y_ref, f32[512,128]{1,0:T(8,128)S(1)} %collective-permute-done.10.c_ref, f32[1024,128]{1,0:T(8,128)S(1)} %slice_dynamic-update-slice_fusion.o_ref, f32[2,1024]{1,0:T(2,128)S(1)} %broadcast_1_prev_ref.2.prev_ref), custom_call_target="tpu_custom_call" | custom-call | flops 805306368 | bytes 2621440 | tf_op jit(solution)/shard_map/pallas_call | solution.py:102
  65.1 0.1 collective-permute-start.8
  65.1 1.1 %shard_map.63.prev_ref = f32[2,1024]{1,0:T(2,128)S(1)} custom-call(f32[1024,2048]{1,0:T(8,128)S(1)} %copy-done, f32[512,128]{1,0:T(8,128)S(1)} %collective-permute-done.17.y_ref, f32[512,128]{1,0:T(8,128)S(1)} %collective-permute-done.18.c_ref, f32[1024,128]{1,0:T(8,128)S(1)} %slice_dynamic-update-slice_fusion.o_ref, f32[2,1024]{1,0:T(2,128)S(1)} %broadcast_1_prev_ref.2.prev_ref), custom_call_target="tpu_custom_call" | custom-call | flops 805306368 | bytes 2621440 | tf_op jit(solution)/shard_map/pallas_call | solution.py:102
  66.2 0.0 collective-permute-done.16.c_ref
  66.2 0.6 collective-permute-start.6
  66.8 1.1 %shard_map.64.prev_ref = f32[2,1024]{1,0:T(2,128)S(1)} custom-call(f32[1024,2048]{1,0:T(8,128)S(1)} %copy-done, f32[512,128]{1,0:T(8,128)S(1)} %collective-permute-done.15.y_ref, f32[512,128]{1,0:T(8,128)S(1)} %collective-permute-done.16.c_ref, f32[1024,128]{1,0:T(8,128)S(1)} %slice_dynamic-update-slice_fusion.o_ref, f32[2,1024]{1,0:T(2,128)S(1)} %shard_map.63.prev_ref), custom_call_target="tpu_custom_call" | custom-call | flops 805306368 | bytes 2621440 | tf_op jit(solution)/shard_map/pallas_call | solution.py:102
  67.9 0.0 collective-permute-done.14.c_ref
  67.9 0.1 collective-permute-start.1
  68.0 1.1 %shard_map.65.prev_ref = f32[2,1024]{1,0:T(2,128)S(1)} custom-call(f32[1024,2048]{1,0:T(8,128)S(1)} %copy-done, f32[512,128]{1,0:T(8,128)S(1)} %collective-permute-done.13.y_ref, f32[512,128]{1,0:T(8,128)S(1)} %collective-permute-done.14.c_ref, f32[1024,128]{1,0:T(8,128)S(1)} %slice_dynamic-update-slice_fusion.o_ref, f32[2,1024]{1,0:T(2,128)S(1)} %shard_map.64.prev_ref), custom_call_target="tpu_custom_call" | custom-call | flops 805306368 | bytes 2621440 | tf_op jit(solution)/shard_map/pallas_call | solution.py:102
  69.1 1.1 %shard_map.66 = f32[2,1024]{1,0:T(2,128)S(1)} custom-call(f32[1024,2048]{1,0:T(8,128)S(1)} %copy-done, f32[512,128]{1,0:T(8,128)S(1)} %collective-permute-done.11.y_ref, f32[512,128]{1,0:T(8,128)S(1)} %collective-permute-done.12.c_ref, f32[1024,128]{1,0:T(8,128)S(1)} %slice_dynamic-update-slice_fusion.o_ref, f32[2,1024]{1,0:T(2,128)S(1)} %shard_map.65.prev_ref), custom_call_target="tpu_custom_call" | custom-call | flops 805306368 | bytes 2621440 | tf_op jit(solution)/shard_map/pallas_call | solution.py:102
  70.2 0.0 collective-permute-done.8.c_ref
  70.2 1.1 %shard_map.60.prev_ref = f32[2,1024]{1,0:T(2,128)S(1)} custom-call(f32[1024,2048]{1,0:T(8,128)S(1)} %copy-done, f32[512,128]{1,0:T(8,128)S(1)} %collective-permute-done.7.y_ref, f32[512,128]{1,0:T(8,128)S(1)} %collective-permute-done.8.c_ref, f32[1024,128]{1,0:T(8,128)S(1)} %slice_dynamic-update-slice_fusion.o_ref, f32[2,1024]{1,0:T(2,128)S(1)} %shard_map.59.prev_ref), custom_call_target="tpu_custom_call" | custom-call | flops 805306368 | bytes 2621440 | tf_op jit(solution)/shard_map/pallas_call | solution.py:102
  71.3 1.1 %shard_map.61.prev_ref = f32[2,1024]{1,0:T(2,128)S(1)} custom-call(f32[1024,2048]{1,0:T(8,128)S(1)} %copy-done, f32[512,128]{1,0:T(8,128)S(1)} %collective-permute-done.5.y_ref, f32[512,128]{1,0:T(8,128)S(1)} %collective-permute-done.6.c_ref, f32[1024,128]{1,0:T(8,128)S(1)} %slice_dynamic-update-slice_fusion.o_ref, f32[2,1024]{1,0:T(2,128)S(1)} %shard_map.60.prev_ref), custom_call_target="tpu_custom_call" | custom-call | flops 805306368 | bytes 2621440 | tf_op jit(solution)/shard_map/pallas_call | solution.py:102
  72.3 0.0 copy-start.1
  72.4 1.1 %shard_map.62 = f32[2,1024]{1,0:T(2,128)S(1)} custom-call(f32[1024,2048]{1,0:T(8,128)S(1)} %copy-done, f32[512,128]{1,0:T(8,128)S(1)} %collective-permute-done.y_ref, f32[512,128]{1,0:T(8,128)S(1)} %collective-permute-done.1.c_ref, f32[1024,128]{1,0:T(8,128)S(1)} %slice_dynamic-update-slice_fusion.o_ref, f32[2,1024]{1,0:T(2,128)S(1)} %shard_map.61.prev_ref), custom_call_target="tpu_custom_call" | custom-call | flops 805306368 | bytes 2621440 | tf_op jit(solution)/shard_map/pallas_call | solution.py:102
  73.5 0.5 copy-done.1
  73.9 9.4 %shard_map.67 = f32[4,1024]{1,0:T(4,128)S(1)} custom-call(f32[1024,2048]{1,0:T(8,128)S(1)} %copy-done, f32[2,2048,128]{2,1,0:T(8,128)S(1)} %copy-done.1, f32[2,2048,128]{2,1,0:T(8,128)S(1)} %collective-permute-done.19.c_ref, f32[1024,128]{1,0:T(8,128)S(1)} %slice_dynamic-update-slice_fusion.o_ref), custom_call_target="tpu_custom_call" | custom-call | flops 6442450944 | bytes 12582912 | tf_op jit(solution)/shard_map/pallas_call | solution.py:58
  83.4 0.4 fusion
  83.8 0.6 collective-permute-start.20
  84.4 0.8 collective-permute-done.20
  85.2 1.7 %collective-permute-start.21 = (f32[8,32]{1,0:T(8,128)S(1)}, f32[8,32]{1,0:T(8,128)S(1)}, u32[]{:S(2)}, u32[]{:S(2)}) collective-permute-start(f32[8,32]{1,0:T(8,128)S(1)} %fusion.5), channel_id=1, source_target_pairs={{0,8},{4,12},{8,0},{12,4},{1,9},{5,13},{9,1},{13,5},{2,10},{6,14},... | collective-permute-start | bytes 3080 | tf_op jit(solution)/shard_map/ppermute | solution.py:178
  86.9 1.9 %collective-permute-done.21 = f32[8,32]{1,0:T(8,128)S(1)} collective-permute-done((f32[8,32]{1,0:T(8,128)S(1)}, f32[8,32]{1,0:T(8,128)S(1)}, u32[]{:S(2)}, u32[]{:S(2)}) %collective-permute-start.21) | collective-permute-done | bytes 1056 | tf_op jit(solution)/shard_map/ppermute | solution.py:178
  88.8 2.4 %collective-permute-start.22 = (f32[8,544]{1,0:T(8,128)S(1)}, f32[8,544]{1,0:T(8,128)S(1)}, u32[]{:S(2)}, u32[]{:S(2)}) collective-permute-start(f32[8,544]{1,0:T(8,128)S(1)} %pad_maximum_fusion.2), channel_id=1, source_target_pairs={{0,2},{1,3},{2,0},{3,1},{4,6},{5,7},{6,4},{7,5},{8,10},{9,11},{10,... | collective-permute-start | bytes 52232 | tf_op jit(solution)/shard_map/ppermute | solution.py:186
  91.2 2.4 %collective-permute-done.22 = f32[8,544]{1,0:T(8,128)S(1)} collective-permute-done((f32[8,544]{1,0:T(8,128)S(1)}, f32[8,544]{1,0:T(8,128)S(1)}, u32[]{:S(2)}, u32[]{:S(2)}) %collective-permute-start.22) | collective-permute-done | bytes 17440 | tf_op jit(solution)/shard_map/ppermute | solution.py:186
  93.6 1.5 %collective-permute-start.23 = (f32[8,288]{1,0:T(8,128)S(1)}, f32[8,288]{1,0:T(8,128)S(1)}, u32[]{:S(2)}, u32[]{:S(2)}) collective-permute-start(f32[8,288]{1,0:T(8,128)S(1)} %pad_maximum_fusion.3), channel_id=1, source_target_pairs={{0,1},{1,0},{2,3},{3,2},{4,5},{5,4},{6,7},{7,6},{8,9},{9,8},{10,11... | collective-permute-start | bytes 27656 | tf_op jit(solution)/shard_map/ppermute | solution.py:186
  95.1 2.3 %collective-permute-done.23 = f32[8,288]{1,0:T(8,128)S(1)} collective-permute-done((f32[8,288]{1,0:T(8,128)S(1)}, f32[8,288]{1,0:T(8,128)S(1)}, u32[]{:S(2)}, u32[]{:S(2)}) %collective-permute-start.23) | collective-permute-done | bytes 9248 | tf_op jit(solution)/shard_map/ppermute | solution.py:186
  97.4 0.7 multiply_bitcast_fusion
  98.0 0.6 fusion.2
  (35 shorter events, 0.3 us)
Async XLA Ops:
  2.9 9.9 %copy-start.3 = (s32[256]{0:T(256)S(1)}, s32[256]{0:T(256)}, u32[]{:S(2)}) copy-start(s32[256]{0:T(256)} %param.7) | copy-start | bytes 3076
  2.9 10.2 %copy-start.2 = (f32[256,128]{1,0:T(8,128)S(1)}, f32[256,128]{1,0:T(8,128)}, u32[]{:S(2)}) copy-start(f32[256,128]{1,0:T(8,128)} %param.6) | copy-start | bytes 393220
  2.9 16.5 %collective-permute-start.4 = (f32[258,128]{1,0:T(8,128)}, f32[258,128]{1,0:T(8,128)}, u32[]{:S(2)}, u32[]{:S(2)}) collective-permute-start(f32[258,128]{1,0:T(8,128)} %pad_maximum_fusion), channel_id=1, source_target_pairs={{0,3},{1,2},{2,1},{3,0},{4,7},{5,6},{6,5},{7,4},{8,11},{9,10},{10,... | collective-permute-start | bytes 396296 | tf_op jit(solution)/shard_map/ppermute | solution.py:142
  7.9 12.1 %collective-permute-start.3 = (f32[258,128]{1,0:T(8,128)}, f32[258,128]{1,0:T(8,128)}, u32[]{:S(2)}, u32[]{:S(2)}) collective-permute-start(f32[258,128]{1,0:T(8,128)} %pad_maximum_fusion), channel_id=1, source_target_pairs={{0,2},{1,3},{2,0},{3,1},{4,6},{5,7},{6,4},{7,5},{8,10},{9,11},{10,... | collective-permute-start | bytes 396296 | tf_op jit(solution)/shard_map/ppermute | solution.py:142
  7.9 9.0 %collective-permute-start.2 = (f32[258,128]{1,0:T(8,128)}, f32[258,128]{1,0:T(8,128)}, u32[]{:S(2)}, u32[]{:S(2)}) collective-permute-start(f32[258,128]{1,0:T(8,128)} %pad_maximum_fusion), channel_id=1, source_target_pairs={{0,1},{1,0},{2,3},{3,2},{4,5},{5,4},{6,7},{7,6},{8,9},{9,8},{10,11... | collective-permute-start | bytes 396296 | tf_op jit(solution)/shard_map/ppermute | solution.py:142
  8.6 64.9 %collective-permute-start.19 = (f32[2,2048,128]{2,1,0:T(8,128)}, f32[2,2048,128]{2,1,0:T(8,128)S(1)}, u32[]{:S(2)}, u32[]{:S(2)}) collective-permute-start(f32[2,2048,128]{2,1,0:T(8,128)} %g_ref.1), channel_id=1, source_target_pairs={{0,4},{4,0},{8,12},{12,8},{1,5},{5,1},{9,13},{13,9},{2,6},{6,2},{1... | collective-permute-start | bytes 6291464 | tf_op jit(solution)/shard_map/ppermute | solution.py:121
  11.1 11.3 %collective-permute-start.9 = (f32[512,128]{1,0:T(8,128)}, f32[512,128]{1,0:T(8,128)S(1)}, u32[]{:S(2)}, u32[]{:S(2)}) collective-permute-start(f32[512,128]{1,0:T(8,128)} %get-tuple-element.2), channel_id=1, source_target_pairs={{0,8},{4,12},{8,0},{12,4},{1,9},{5,13},{9,1},{13,5},{2,10},{6,14},... | collective-permute-start | bytes 786440 | tf_op jit(solution)/shard_map/ppermute | solution.py:133
  16.9 9.5 %collective-permute-start.17 = (f32[512,128]{1,0:T(8,128)}, f32[512,128]{1,0:T(8,128)S(1)}, u32[]{:S(2)}, u32[]{:S(2)}) collective-permute-start(f32[512,128]{1,0:T(8,128)} %get-tuple-element.3), channel_id=1, source_target_pairs={{0,8},{4,12},{8,0},{12,4},{1,9},{5,13},{9,1},{13,5},{2,10},{6,14},... | collective-permute-start | bytes 786440 | tf_op jit(solution)/shard_map/ppermute | solution.py:133
  19.4 12.6 %collective-permute-start.15 = (f32[512,128]{1,0:T(8,128)}, f32[512,128]{1,0:T(8,128)S(1)}, u32[]{:S(2)}, u32[]{:S(2)}) collective-permute-start(f32[512,128]{1,0:T(8,128)} %get-tuple-element.4), channel_id=1, source_target_pairs={{0,8},{4,12},{8,0},{12,4},{1,9},{5,13},{9,1},{13,5},{2,10},{6,14},... | collective-permute-start | bytes 786440 | tf_op jit(solution)/shard_map/ppermute | solution.py:133
  20.0 17.6 %collective-permute-start.13 = (f32[512,128]{1,0:T(8,128)}, f32[512,128]{1,0:T(8,128)S(1)}, u32[]{:S(2)}, u32[]{:S(2)}) collective-permute-start(f32[512,128]{1,0:T(8,128)} %get-tuple-element.5), channel_id=1, source_target_pairs={{0,8},{4,12},{8,0},{12,4},{1,9},{5,13},{9,1},{13,5},{2,10},{6,14},... | collective-permute-start | bytes 786440 | tf_op jit(solution)/shard_map/ppermute | solution.py:133
  22.4 20.8 %collective-permute-start.11 = (f32[512,128]{1,0:T(8,128)S(1)}, f32[512,128]{1,0:T(8,128)S(1)}, u32[]{:S(2)}, u32[]{:S(2)}) collective-permute-start(f32[512,128]{1,0:T(8,128)S(1)} %get-tuple-element.6), channel_id=1, source_target_pairs={{0,8},{4,12},{8,0},{12,4},{1,9},{5,13},{9,1},{13,5},{2,10},{6,14},... | collective-permute-start | bytes 786440 | tf_op jit(solution)/shard_map/ppermute | solution.py:133
  26.4 22.5 %collective-permute-start.7 = (f32[512,128]{1,0:T(8,128)S(1)}, f32[512,128]{1,0:T(8,128)S(1)}, u32[]{:S(2)}, u32[]{:S(2)}) collective-permute-start(f32[512,128]{1,0:T(8,128)S(1)} %get-tuple-element.7), channel_id=1, source_target_pairs={{0,8},{4,12},{8,0},{12,4},{1,9},{5,13},{9,1},{13,5},{2,10},{6,14},... | collective-permute-start | bytes 786440 | tf_op jit(solution)/shard_map/ppermute | solution.py:133
  32.0 22.5 %collective-permute-start.5 = (f32[512,128]{1,0:T(8,128)S(1)}, f32[512,128]{1,0:T(8,128)S(1)}, u32[]{:S(2)}, u32[]{:S(2)}) collective-permute-start(f32[512,128]{1,0:T(8,128)S(1)} %get-tuple-element.8), channel_id=1, source_target_pairs={{0,8},{4,12},{8,0},{12,4},{1,9},{5,13},{9,1},{13,5},{2,10},{6,14},... | collective-permute-start | bytes 786440 | tf_op jit(solution)/shard_map/ppermute | solution.py:133
  37.6 21.7 %collective-permute-start = (f32[512,128]{1,0:T(8,128)S(1)}, f32[512,128]{1,0:T(8,128)S(1)}, u32[]{:S(2)}, u32[]{:S(2)}) collective-permute-start(f32[512,128]{1,0:T(8,128)S(1)} %get-tuple-element.9), channel_id=1, source_target_pairs={{0,8},{4,12},{8,0},{12,4},{1,9},{5,13},{9,1},{13,5},{2,10},{6,14},... | collective-permute-start | bytes 786440 | tf_op jit(solution)/shard_map/ppermute | solution.py:133
  43.2 16.8 %collective-permute-start.10 = (f32[512,128]{1,0:T(8,128)S(1)}, f32[512,128]{1,0:T(8,128)S(1)}, u32[]{:S(2)}, u32[]{:S(2)}) collective-permute-start(f32[512,128]{1,0:T(8,128)S(1)} %collective-permute-done.9.y_ref), channel_id=1, source_target_pairs={{0,4},{4,0},{8,12},{12,8},{1,5},{5,1},{9,13},{13,9},{2,6},{6,2},{1... | collective-permute-start | bytes 786440 | tf_op jit(solution)/shard_map/ppermute | solution.py:121
  48.9 16.2 %collective-permute-start.18 = (f32[512,128]{1,0:T(8,128)S(1)}, f32[512,128]{1,0:T(8,128)S(1)}, u32[]{:S(2)}, u32[]{:S(2)}) collective-permute-start(f32[512,128]{1,0:T(8,128)S(1)} %collective-permute-done.17.y_ref), channel_id=1, source_target_pairs={{0,4},{4,0},{8,12},{12,8},{1,5},{5,1},{9,13},{13,9},{2,6},{6,2},{1... | collective-permute-start | bytes 786440 | tf_op jit(solution)/shard_map/ppermute | solution.py:121
  54.5 11.8 %collective-permute-start.16 = (f32[512,128]{1,0:T(8,128)S(1)}, f32[512,128]{1,0:T(8,128)S(1)}, u32[]{:S(2)}, u32[]{:S(2)}) collective-permute-start(f32[512,128]{1,0:T(8,128)S(1)} %collective-permute-done.15.y_ref), channel_id=1, source_target_pairs={{0,4},{4,0},{8,12},{12,8},{1,5},{5,1},{9,13},{13,9},{2,6},{6,2},{1... | collective-permute-start | bytes 786440 | tf_op jit(solution)/shard_map/ppermute | solution.py:121
  59.4 8.5 %collective-permute-start.14 = (f32[512,128]{1,0:T(8,128)S(1)}, f32[512,128]{1,0:T(8,128)S(1)}, u32[]{:S(2)}, u32[]{:S(2)}) collective-permute-start(f32[512,128]{1,0:T(8,128)S(1)} %collective-permute-done.13.y_ref), channel_id=1, source_target_pairs={{0,4},{4,0},{8,12},{12,8},{1,5},{5,1},{9,13},{13,9},{2,6},{6,2},{1... | collective-permute-start | bytes 786440 | tf_op jit(solution)/shard_map/ppermute | solution.py:121
  60.1 9.0 %collective-permute-start.12 = (f32[512,128]{1,0:T(8,128)S(1)}, f32[512,128]{1,0:T(8,128)S(1)}, u32[]{:S(2)}, u32[]{:S(2)}) collective-permute-start(f32[512,128]{1,0:T(8,128)S(1)} %collective-permute-done.11.y_ref), channel_id=1, source_target_pairs={{0,4},{4,0},{8,12},{12,8},{1,5},{5,1},{9,13},{13,9},{2,6},{6,2},{1... | collective-permute-start | bytes 786440 | tf_op jit(solution)/shard_map/ppermute | solution.py:121
  60.6 3.4 %copy-start = (f32[1024,2048]{1,0:T(8,128)S(1)}, f32[1024,2048]{1,0:T(8,128)}, u32[]{:S(2)}) copy-start(f32[1024,2048]{1,0:T(8,128)} %a_ref.17) | copy-start | bytes 25165828
  65.1 5.1 %collective-permute-start.8 = (f32[512,128]{1,0:T(8,128)S(1)}, f32[512,128]{1,0:T(8,128)S(1)}, u32[]{:S(2)}, u32[]{:S(2)}) collective-permute-start(f32[512,128]{1,0:T(8,128)S(1)} %collective-permute-done.7.y_ref), channel_id=1, source_target_pairs={{0,4},{4,0},{8,12},{12,8},{1,5},{5,1},{9,13},{13,9},{2,6},{6,2},{1... | collective-permute-start | bytes 786440 | tf_op jit(solution)/shard_map/ppermute | solution.py:121
  66.2 5.0 %collective-permute-start.6 = (f32[512,128]{1,0:T(8,128)S(1)}, f32[512,128]{1,0:T(8,128)S(1)}, u32[]{:S(2)}, u32[]{:S(2)}) collective-permute-start(f32[512,128]{1,0:T(8,128)S(1)} %collective-permute-done.5.y_ref), channel_id=1, source_target_pairs={{0,4},{4,0},{8,12},{12,8},{1,5},{5,1},{9,13},{13,9},{2,6},{6,2},{1... | collective-permute-start | bytes 786440 | tf_op jit(solution)/shard_map/ppermute | solution.py:121
  67.9 4.5 %collective-permute-start.1 = (f32[512,128]{1,0:T(8,128)S(1)}, f32[512,128]{1,0:T(8,128)S(1)}, u32[]{:S(2)}, u32[]{:S(2)}) collective-permute-start(f32[512,128]{1,0:T(8,128)S(1)} %collective-permute-done.y_ref), channel_id=1, source_target_pairs={{0,4},{4,0},{8,12},{12,8},{1,5},{5,1},{9,13},{13,9},{2,6},{6,2},{1... | collective-permute-start | bytes 786440 | tf_op jit(solution)/shard_map/ppermute | solution.py:121
  72.3 1.6 %copy-start.1 = (f32[2,2048,128]{2,1,0:T(8,128)S(1)}, f32[2,2048,128]{2,1,0:T(8,128)}, u32[]{:S(2)}) copy-start(f32[2,2048,128]{2,1,0:T(8,128)} %g_ref.1) | copy-start | bytes 6291460
  83.8 1.4 %collective-permute-start.20 = (f32[8,32]{1,0:T(8,128)S(1)}, f32[8,32]{1,0:T(8,128)S(1)}, u32[]{:S(2)}, u32[]{:S(2)}) collective-permute-start(f32[8,32]{1,0:T(8,128)S(1)} %pad_maximum_fusion.6), channel_id=1, source_target_pairs={{0,4},{4,0},{8,12},{12,8},{1,5},{5,1},{9,13},{13,9},{2,6},{6,2},{1... | collective-permute-start | bytes 3080 | tf_op jit(solution)/shard_map/ppermute | solution.py:178
  85.2 3.6 %collective-permute-start.21 = (f32[8,32]{1,0:T(8,128)S(1)}, f32[8,32]{1,0:T(8,128)S(1)}, u32[]{:S(2)}, u32[]{:S(2)}) collective-permute-start(f32[8,32]{1,0:T(8,128)S(1)} %fusion.5), channel_id=1, source_target_pairs={{0,8},{4,12},{8,0},{12,4},{1,9},{5,13},{9,1},{13,5},{2,10},{6,14},... | collective-permute-start | bytes 3080 | tf_op jit(solution)/shard_map/ppermute | solution.py:178
  88.8 4.7 %collective-permute-start.22 = (f32[8,544]{1,0:T(8,128)S(1)}, f32[8,544]{1,0:T(8,128)S(1)}, u32[]{:S(2)}, u32[]{:S(2)}) collective-permute-start(f32[8,544]{1,0:T(8,128)S(1)} %pad_maximum_fusion.2), channel_id=1, source_target_pairs={{0,2},{1,3},{2,0},{3,1},{4,6},{5,7},{6,4},{7,5},{8,10},{9,11},{10,... | collective-permute-start | bytes 52232 | tf_op jit(solution)/shard_map/ppermute | solution.py:186
  93.6 3.8 %collective-permute-start.23 = (f32[8,288]{1,0:T(8,128)S(1)}, f32[8,288]{1,0:T(8,128)S(1)}, u32[]{:S(2)}, u32[]{:S(2)}) collective-permute-start(f32[8,288]{1,0:T(8,128)S(1)} %pad_maximum_fusion.3), channel_id=1, source_target_pairs={{0,1},{1,0},{2,3},{3,2},{4,5},{5,4},{6,7},{7,6},{8,9},{9,8},{10,11... | collective-permute-start | bytes 27656 | tf_op jit(solution)/shard_map/ppermute | solution.py:186
